TPU v7x, 512 devices: a whole 4x4x16 slice. The times are simulated.
512 devices in a mesh: expert: 64 (over z, y), replica: 8 (over x, core).
Axes of the slice: x: 4, y: 4, z: 16, core: 2. Of those that a mesh axis runs over, the one named last changes fastest.
Arguments:
- cotangent: bfloat16 [65536, 2048], P(('expert', 'replica')), may hold values from -2 to 2
- hidden: bfloat16 [65536, 6, 704], P(('expert', 'replica')), may hold values from -24 to 24
- routes: int32 [65536, 6], P(('expert', 'replica')), may hold values from 0 to 63, all different within a row; in each aligned block of 128 rows (0 to 127, 128 to 255, ...) at most 18 rows name the same one
- numerators: int32 [65536, 6], P(('expert', 'replica')), may hold values from 1 to 1024
- w_down: bfloat16 [64, 704, 2048], P('expert'), may hold values from -0.21875 to 0.21875
Outputs:
- gate_grad: float32 [65536, 6], P(('expert', 'replica'))
- grad_scales: float32 [64, 704, 16], P('expert', 'replica')
- grad_mantissa: float32 [64, 704, 2048], P('expert', 'replica')
Inputs may be any that keep to these rules, and one draw needn't show every extreme that they name: `routes`: no expert is named by more than 18 rows of one device's tokens, a bound that some blocks reach.
All inputs are finite; a program needn't handle non-finite values. Where the computation divides by a largest or mean magnitude, that divisor is 1e-20 or more.
Results may differ from a plain program's by a relative error of at most 0.023.
Values may be sent and summed in bfloat16 or wider, within the bound.
A program may use at most 64 MiB of HBM per device.

v0:
```python
import jax
import jax.numpy as jnp
from jax import lax
from jax.sharding import PartitionSpec as P

BLOCK = 128


def per_device(cotangent, hidden, routes, numerators, w_down):
    tok_count = cotangent.shape[0]
    model_width = cotangent.shape[1]
    top_k = hidden.shape[1]
    hidden_width = hidden.shape[2]
    experts = lax.axis_size("expert")
    replicas = lax.axis_size("replica")
    slot_count = 3 * tok_count * top_k // (2 * experts)
    routed = tok_count * top_k
    total_slots = experts * slot_count
    flat_routes = routes.reshape(routed)
    one_hot = (flat_routes[:, None] == jnp.arange(experts, dtype=jnp.int32)[None, :]).astype(
        jnp.int32
    )
    before = jnp.cumsum(one_hot, axis=0) - one_hot
    rank_in = jnp.sum(before * one_hot, axis=1)
    slot_of = flat_routes * slot_count + rank_in
    source_row = (
        jnp.full((total_slots,), routed, jnp.int32)
        .at[slot_of]
        .set(jnp.arange(routed, dtype=jnp.int32))
    )
    in_use = source_row < routed
    token_row = jnp.where(in_use, source_row // top_k, tok_count)
    padded_cot = jnp.concatenate([cotangent, jnp.zeros((1, model_width), cotangent.dtype)], axis=0)
    send_cot = padded_cot[token_row].reshape(experts, slot_count, model_width)
    padded_hid = jnp.concatenate(
        [hidden.reshape(routed, hidden_width), jnp.zeros((1, hidden_width), hidden.dtype)], axis=0
    )
    send_hid = padded_hid[source_row].reshape(experts, slot_count, hidden_width)
    weights_flat = numerators.reshape(routed).astype(jnp.float32) / 1024.0
    padded_w = jnp.concatenate([weights_flat, jnp.zeros((1,), jnp.float32)], axis=0)
    send_w = padded_w[source_row].reshape(experts, slot_count)
    matrix = w_down[0]
    contract_width = (((1,), (1,)), ((), ()))
    got_cot, got_w, got_hid = (
        lax.all_to_all(send_cot, "expert", split_axis=0, concat_axis=0, tiled=True),
        lax.all_to_all(
            send_w.astype(jnp.bfloat16), "expert", split_axis=0, concat_axis=0, tiled=True
        ).astype(send_w.dtype),
        lax.all_to_all(send_hid, "expert", split_axis=0, concat_axis=0, tiled=True),
    )
    cot_flat = got_cot.reshape(total_slots, model_width)
    back_proj = lax.dot_general(
        cot_flat, matrix, contract_width, preferred_element_type=jnp.float32
    )
    hid_flat = got_hid.reshape(total_slots, hidden_width)
    gate_local = jnp.sum(back_proj * hid_flat.astype(jnp.float32), axis=1)
    returned = lax.all_to_all(
        gate_local.reshape(experts, slot_count), "expert", split_axis=0, concat_axis=0, tiled=True
    )
    gate_grad = returned.reshape(total_slots)[slot_of].reshape(tok_count, top_k)
    scaled = (got_w.reshape(total_slots)[:, None] * cot_flat.astype(jnp.float32)).astype(
        jnp.bfloat16
    )
    partial_value = lax.dot_general(
        hid_flat, scaled, (((0,), (0,)), ((), ())), preferred_element_type=jnp.float32
    )
    blocks = partial_value.reshape(hidden_width, model_width // BLOCK, BLOCK)
    local_max = jnp.max(jnp.abs(blocks), axis=2)
    scales = lax.pmax(local_max.astype(jnp.bfloat16), "replica").astype(local_max.dtype) + 1e-06
    mantissa = (blocks / scales[:, :, None]).astype(jnp.bfloat16)
    mantissa = (
        lax.optimization_barrier(mantissa).astype(jnp.float32).reshape(hidden_width, model_width)
    )
    share_rows = hidden_width // replicas
    share_start = lax.axis_index("replica") * share_rows
    whole_sum = lax.psum(mantissa.astype(jnp.bfloat16), "replica").astype(jnp.float32)
    summed = lax.dynamic_slice_in_dim(whole_sum, share_start, share_rows, 0)
    scale_share = lax.dynamic_slice_in_dim(scales, share_start, share_rows, 0)
    return (gate_grad, scale_share[None], summed[None])


def solution(mesh):
    return jax.shard_map(
        per_device,
        mesh=mesh,
        in_specs=(
            P(("expert", "replica"), None),
            P(("expert", "replica"), None, None),
            P(("expert", "replica"), None),
            P(("expert", "replica"), None),
            P("expert", None, None),
        ),
        out_specs=(
            P(("expert", "replica"), None),
            P("expert", "replica", None),
            P("expert", "replica", None),
        ),
        check_vma=False,
    )
```

profile of v0, /device:TPU:8, one launch (start us, length us, event | category | flops | bytes accessed | tf_op | source)
XLA Modules:
  0.0 615.8 jit_solution(7978967521401818478)
XLA Ops:
  11.7 3.4 scatter_custom_fusion
  16.1 7.3 %gather_fusion.3 = bf16[1152]{0:T(1024)(128)(2,1)S(1)} fusion(bf16[769]{0:T(1024)(128)(2,1)S(1)} %pad_maximum_fusion, s32[2048]{0:T(1024)S(1)} %get-tuple-element.13), kind=kCustom, calls=%fused_computation.3 | custom fusion | bytes 9216 | tf_op jit(solution)/shard_map/gather | solution.py:41
  24.2 18.7 %all-to-all-start.3 = ((bf16[64,1,18]{2,1,0:T(2,128)(2,1)}), bf16[64,1,18]{2,1,0:T(2,128)(2,1)S(1)}, u32[]{:S(2)}, u32[]{:S(2)}) async-start(bf16[64,1,18]{2,1,0:T(2,128)(2,1)} %convert_element_type.76), calls=%async_computation.3 | async-start | bytes 65536 | tf_op jit(solution)/shard_map/all_to_all | solution.py:46
  51.5 7.1 %gather_fusion.1 = bf16[1152,704]{1,0:T(8,128)(2,1)} fusion(bf16[769,704]{1,0:T(8,128)(2,1)} %concatenate.10, s32[2048]{0:T(1024)S(1)} %get-tuple-element.13), kind=kCustom, calls=%fused_computation.1 | custom fusion | bytes 3248640 | tf_op jit(solution)/shard_map/gather | solution.py:38
  58.7 4.1 reshape.112
  62.8 15.3 %all-to-all-start.1 = ((bf16[64,18,704]{2,1,0:T(8,128)(2,1)}), bf16[64,18,704]{2,1,0:T(8,128)(2,1)}, u32[]{:S(2)}, u32[]{:S(2)}) async-start(bf16[64,18,704]{2,1,0:T(8,128)(2,1)} %reshape.112), calls=%async_computation.1 | async-start | bytes 4718592 | tf_op jit(solution)/shard_map/all_to_all | solution.py:49
  79.1 6.0 gather_fusion
  85.1 7.5 %reshape.109 = bf16[64,18,2048]{2,1,0:T(8,128)(2,1)} reshape(bf16[1152,2048]{1,0:T(8,128)(2,1)} %gather_fusion) | data formatting | bytes 9437184 | tf_op jit(solution)/shard_map/reshape | solution.py:34
  92.6 96.1 %all-to-all-done.1 = bf16[64,18,704]{2,1,0:T(8,128)(2,1)} async-done(((bf16[64,18,704]{2,1,0:T(8,128)(2,1)}), bf16[64,18,704]{2,1,0:T(8,128)(2,1)}, u32[]{:S(2)}, u32[]{:S(2)}) %all-to-all-start.1) | async-done | bytes 1622048 | tf_op jit(solution)/shard_map/all_to_all | solution.py:49
  188.8 6.1 all-to-all-start
  195.3 4.1 reshape.113
  199.5 274.3 %all-to-all-done = bf16[64,18,2048]{2,1,0:T(8,128)(2,1)} async-done(((bf16[64,18,2048]{2,1,0:T(8,128)(2,1)}), bf16[64,18,2048]{2,1,0:T(8,128)(2,1)}, u32[]{:S(2)}, u32[]{:S(2)}) %all-to-all-start) | async-done | bytes 4718624 | tf_op jit(solution)/shard_map/all_to_all | solution.py:45
  473.8 7.7 %reshape.110 = bf16[1152,2048]{1,0:T(8,128)(2,1)} reshape(bf16[64,18,2048]{2,1,0:T(8,128)(2,1)} %all-to-all-done) | data formatting | bytes 9437184 | tf_op jit(solution)/shard_map/reshape | solution.py:51
  481.4 5.4 fusion
  486.8 6.8 %copy.37 = bf16[2048,1152]{1,0:T(8,128)(2,1)} copy(bf16[2048,1152]{0,1:T(8,128)(2,1)} %fusion) | data formatting | bytes 9437184 | tf_op jit(solution)/shard_map/dot_general | solution.py:64
  493.6 9.0 %abs_reduce_fusion = (bf16[704,16]{0,1:T(8,128)(2,1)S(1)}, f32[704,16,128]{2,0,1:T(8,128)}) fusion(bf16[16,128,1152]{2,1,0:T(8,128)(2,1)} %bitcast.45, bf16[1152,704]{1,0:T(8,128)(2,1)} %reshape.113), kind=kOutput, calls=%fused_computation.7 | convolution fusion | flops 3326202880 | bytes 12130304 | tf_op jit(solution)/shard_map/dot_general | solution.py:64
  502.6 23.6 %pmax.7 = bf16[704,16]{0,1:T(8,128)(2,1)S(1)} all-reduce(bf16[704,16]{0,1:T(8,128)(2,1)S(1)} %get-tuple-element.11), channel_id=1, replica_groups=mesh['expert'=64,'replica'=8] {'replica'}, use_global_device_ids=true, to_apply=%region_6.7 | all-reduce | flops 11264 | bytes 45056 | tf_op jit(solution)/shard_map/pmax | solution.py:69
  526.2 4.3 divide_convert_fusion
  532.5 3.8 copy.27
  536.3 6.8 %fusion.4 = f32[1152]{0:T(1024)S(1)} fusion(bf16[1152,704]{0,1:T(8,128)(2,1)} %copy.27, bf16[1152,2048]{1,0:T(8,128)(2,1)} %reshape.110, bf16[1,704,2048]{2,1,0:T(8,128)(2,1)S(1)} %copy-done), kind=kOutput, calls=%fused_computation.14 | convolution fusion | flops 3324320768 | bytes 9228800 | tf_op jit(solution)/shard_map/dot_general | solution.py:52
  543.9 7.3 %all-to-all-start.2 = ((f32[64,1,18]{2,1,0:T(1,128)}), f32[64,1,18]{2,1,0:T(1,128)S(1)}, u32[]{:S(2)}, u32[]{:S(2)}) async-start(f32[64,1,18]{2,1,0:T(1,128)} %bitcast.2), calls=%async_computation.2 | async-start | bytes 65536 | tf_op jit(solution)/shard_map/all_to_all | solution.py:57
  551.9 12.9 %all-to-all-done.2 = f32[64,1,18]{2,1,0:T(1,128)S(1)} async-done(((f32[64,1,18]{2,1,0:T(1,128)}), f32[64,1,18]{2,1,0:T(1,128)S(1)}, u32[]{:S(2)}, u32[]{:S(2)}) %all-to-all-start.2) | async-done | bytes 4640 | tf_op jit(solution)/shard_map/all_to_all | solution.py:57
  566.2 4.5 gather_fusion.2
  571.5 35.6 %all-reduce.4.cloned.1.call-done = bf16[704,2048]{1,0:T(8,128)(2,1)} async-done(((bf16[704,2048]{1,0:T(8,128)(2,1)}), bf16[704,2048]{1,0:T(8,128)(2,1)}) %all-reduce.4.cloned.1.call-update) | async-done | bytes 2883600 | tf_op jit(solution)/shard_map/psum | solution.py:76
  (42 shorter events, 23.9 us)
Async XLA Ops:
  7.2 529.2 %copy-start = (bf16[1,704,2048]{2,1,0:T(8,128)(2,1)S(1)}, bf16[1,704,2048]{2,1,0:T(8,128)(2,1)}, u32[]{:S(2)}) copy-start(bf16[1,704,2048]{2,1,0:T(8,128)(2,1)} %param.9) | copy-start | bytes 8650756
  24.2 38.6 %all-to-all-start.3 = ((bf16[64,1,18]{2,1,0:T(2,128)(2,1)}), bf16[64,1,18]{2,1,0:T(2,128)(2,1)S(1)}, u32[]{:S(2)}, u32[]{:S(2)}) async-start(bf16[64,1,18]{2,1,0:T(2,128)(2,1)} %convert_element_type.76), calls=%async_computation.3 | async-start | bytes 65536 | tf_op jit(solution)/shard_map/all_to_all | solution.py:46
  62.8 126.0 %all-to-all-start.1 = ((bf16[64,18,704]{2,1,0:T(8,128)(2,1)}), bf16[64,18,704]{2,1,0:T(8,128)(2,1)}, u32[]{:S(2)}, u32[]{:S(2)}) async-start(bf16[64,18,704]{2,1,0:T(8,128)(2,1)} %reshape.112), calls=%async_computation.1 | async-start | bytes 4718592 | tf_op jit(solution)/shard_map/all_to_all | solution.py:49
  188.8 285.0 %all-to-all-start = ((bf16[64,18,2048]{2,1,0:T(8,128)(2,1)}), bf16[64,18,2048]{2,1,0:T(8,128)(2,1)}, u32[]{:S(2)}, u32[]{:S(2)}) async-start(bf16[64,18,2048]{2,1,0:T(8,128)(2,1)} %reshape.109), calls=%async_computation | async-start | bytes 12582912 | tf_op jit(solution)/shard_map/all_to_all | solution.py:45
  194.9 412.2 %all-reduce.4.cloned.1.call-start = ((), (), s32[]{:S(2)}) async-start(), calls=%async_computation.4 | async-start | bytes 5767168 | tf_op jit(solution)/shard_map/psum | solution.py:76
  543.9 20.9 %all-to-all-start.2 = ((f32[64,1,18]{2,1,0:T(1,128)}), f32[64,1,18]{2,1,0:T(1,128)S(1)}, u32[]{:S(2)}, u32[]{:S(2)}) async-start(f32[64,1,18]{2,1,0:T(1,128)} %bitcast.2), calls=%async_computation.2 | async-start | bytes 65536 | tf_op jit(solution)/shard_map/all_to_all | solution.py:57
Sparse Core Ops, SparseCore 0:
  532.6 74.3 all-reduce.3
where the time goes:
time: 617 us; the launch traced here: 616 us
  waiting for transfers between devices  419 us (68%)
  local copies, waits for them, and re-layouts  79.6 us (13%)
  starting transfers between devices  47.6 us (8%)
  blocking collectives  23.6 us (4%)
  other arithmetic  15.9 us (3%)
  matrix products  15.8 us (3%)
  between operations  14.2 us (2%)
    all_to_all x1, waiting for transfers between devices, per_device(): lax.all_to_all(send_cot, 'expert', split_axis=0, concat_axis=0, tiled=True)  274 us
    all_to_all x1, waiting for transfers between devices, per_device(): lax.all_to_all(send_hid, 'expert', split_axis=0, concat_axis=0, tiled=True)  96.1 us
    psum x1, waiting for transfers between devices, per_device(): lax.psum(mantissa.astype(jnp.bfloat16), 'replica').astype(jnp.float32)  35.6 us
    pmax x1, blocking collectives, per_device(): lax.pmax(local_max.astype(jnp.bfloat16), 'replica').astype(local_max.dtype)  23.6 us
    all_to_all x1, starting transfers between devices, per_device(): lax.all_to_all(send_w.astype(jnp.bfloat16), 'expert', split_axis=0, conca...  18.7 us
    all_to_all x1, starting transfers between devices, per_device(): lax.all_to_all(send_hid, 'expert', split_axis=0, concat_axis=0, tiled=True)  15.3 us
    all_to_all x1, waiting for transfers between devices, per_device(): lax.all_to_all(gate_local.reshape(experts, slot_count), 'expert', split_a...  12.9 us
  transfers between devices with their start and end apart: 5, of which 4 were waited for; matrix products, arithmetic and copies ran while one was open for 9% of the time, Pallas kernels for 0%

commit v1 on v0

--- a/solution.py
+++ b/solution.py
@@ -73,7 +73,9 @@
     )
     share_rows = hidden_width // replicas
     share_start = lax.axis_index("replica") * share_rows
-    whole_sum = lax.psum(mantissa.astype(jnp.bfloat16), "replica").astype(jnp.float32)
+    whole_sum = jnp.sum(lax.all_gather(mantissa.astype(jnp.bfloat16), "replica"), axis=0).astype(
+        jnp.float32
+    )
     summed = lax.dynamic_slice_in_dim(whole_sum, share_start, share_rows, 0)
     scale_share = lax.dynamic_slice_in_dim(scales, share_start, share_rows, 0)
     return (gate_grad, scale_share[None], summed[None])

time: 617 us -> 676 us (1.096)
  the two profiles are of different devices: /device:TPU:8 before, /device:TPU:1 now
where the time goes in v1:
time: 676 us; the launch traced here: 674 us
  waiting for transfers between devices  446 us (66%)
  local copies, waits for them, and re-layouts  86.9 us (13%)
  starting transfers between devices  52.3 us (8%)
  other arithmetic  30.4 us (4%)
  blocking collectives  28.4 us (4%)
  matrix products  15.9 us (2%)
  between operations  14.2 us (2%)
    all_to_all x1, waiting for transfers between devices, per_device(): lax.all_to_all(send_cot, 'expert', split_axis=0, concat_axis=0, tiled=True)  268 us
    all_to_all x1, waiting for transfers between devices, per_device(): lax.all_to_all(send_hid, 'expert', split_axis=0, concat_axis=0, tiled=True)  90.6 us
    all_gather x1, waiting for transfers between devices, per_device(): lax.all_gather(mantissa.astype(jnp.bfloat16), 'replica')  74.6 us
    pmax x1, blocking collectives, per_device(): lax.pmax(local_max.astype(jnp.bfloat16), 'replica').astype(local_max.dtype)  28.4 us
    all_to_all x1, starting transfers between devices, per_device(): lax.all_to_all(send_w.astype(jnp.bfloat16), 'expert', split_axis=0, conca...  19.3 us
    all_to_all x1, starting transfers between devices, per_device(): lax.all_to_all(send_hid, 'expert', split_axis=0, concat_axis=0, tiled=True)  14.8 us
    reduce_sum x1, other arithmetic, per_device(): jnp.sum(lax.all_gather(mantissa.astype(jnp.bfloat16), 'replica'), axis=0)  14.6 us
  transfers between devices with their start and end apart: 5, of which 4 were waited for; matrix products, arithmetic and copies ran while one was open for 8% of the time, Pallas kernels for 0%

profile of v1, /device:TPU:1, one launch (start us, length us, event | category | flops | bytes accessed | tf_op | source)
XLA Modules:
  0.0 674.0 jit_solution(10540772801046504508)
XLA Ops:
  16.1 7.3 %gather_fusion.3 = bf16[1152]{0:T(1024)(128)(2,1)S(1)} fusion(bf16[769]{0:T(1024)(128)(2,1)S(1)} %pad_maximum_fusion, s32[2048]{0:T(1024)S(1)} %get-tuple-element.13), kind=kCustom, calls=%fused_computation.3 | custom fusion | bytes 9216 | tf_op jit(solution)/shard_map/gather | solution.py:41
  24.2 19.3 %all-to-all-start.3 = ((bf16[64,1,18]{2,1,0:T(2,128)(2,1)}), bf16[64,1,18]{2,1,0:T(2,128)(2,1)S(1)}, u32[]{:S(2)}, u32[]{:S(2)}) async-start(bf16[64,1,18]{2,1,0:T(2,128)(2,1)} %convert_element_type.85), calls=%async_computation.3 | async-start | bytes 65536 | tf_op jit(solution)/shard_map/all_to_all | solution.py:46
  52.2 7.1 %gather_fusion.1 = bf16[1152,704]{1,0:T(8,128)(2,1)} fusion(bf16[769,704]{1,0:T(8,128)(2,1)} %concatenate.10, s32[2048]{0:T(1024)S(1)} %get-tuple-element.13), kind=kCustom, calls=%fused_computation.1 | custom fusion | bytes 3248640 | tf_op jit(solution)/shard_map/gather | solution.py:38
  59.3 4.1 reshape.122
  63.4 14.8 %all-to-all-start.1 = ((bf16[64,18,704]{2,1,0:T(8,128)(2,1)}), bf16[64,18,704]{2,1,0:T(8,128)(2,1)}, u32[]{:S(2)}, u32[]{:S(2)}) async-start(bf16[64,18,704]{2,1,0:T(8,128)(2,1)} %reshape.122), calls=%async_computation.1 | async-start | bytes 4718592 | tf_op jit(solution)/shard_map/all_to_all | solution.py:49
  79.2 6.1 gather_fusion
  85.3 7.6 %reshape.119 = bf16[64,18,2048]{2,1,0:T(8,128)(2,1)} reshape(bf16[1152,2048]{1,0:T(8,128)(2,1)} %gather_fusion) | data formatting | bytes 9437184 | tf_op jit(solution)/shard_map/reshape | solution.py:34
  92.9 90.6 %all-to-all-done.1 = bf16[64,18,704]{2,1,0:T(8,128)(2,1)} async-done(((bf16[64,18,704]{2,1,0:T(8,128)(2,1)}), bf16[64,18,704]{2,1,0:T(8,128)(2,1)}, u32[]{:S(2)}, u32[]{:S(2)}) %all-to-all-start.1) | async-done | bytes 1622048 | tf_op jit(solution)/shard_map/all_to_all | solution.py:49
  183.5 11.1 %all-to-all-start = ((bf16[64,18,2048]{2,1,0:T(8,128)(2,1)}), bf16[64,18,2048]{2,1,0:T(8,128)(2,1)}, u32[]{:S(2)}, u32[]{:S(2)}) async-start(bf16[64,18,2048]{2,1,0:T(8,128)(2,1)} %reshape.119), calls=%async_computation | async-start | bytes 12582912 | tf_op jit(solution)/shard_map/all_to_all | solution.py:45
  195.1 4.1 reshape.123
  199.2 268.0 %all-to-all-done = bf16[64,18,2048]{2,1,0:T(8,128)(2,1)} async-done(((bf16[64,18,2048]{2,1,0:T(8,128)(2,1)}), bf16[64,18,2048]{2,1,0:T(8,128)(2,1)}, u32[]{:S(2)}, u32[]{:S(2)}) %all-to-all-start) | async-done | bytes 4718624 | tf_op jit(solution)/shard_map/all_to_all | solution.py:45
  467.2 7.8 %reshape.120 = bf16[1152,2048]{1,0:T(8,128)(2,1)} reshape(bf16[64,18,2048]{2,1,0:T(8,128)(2,1)} %all-to-all-done) | data formatting | bytes 9437184 | tf_op jit(solution)/shard_map/reshape | solution.py:51
  475.0 5.3 fusion
  480.3 6.7 copy.37
  487.0 9.1 %abs_reduce_fusion = (bf16[704,16]{0,1:T(8,128)(2,1)S(1)}, f32[704,16,128]{2,0,1:T(8,128)}) fusion(bf16[16,128,1152]{2,1,0:T(8,128)(2,1)} %bitcast.40, bf16[1152,704]{1,0:T(8,128)(2,1)} %reshape.123), kind=kOutput, calls=%fused_computation.7 | convolution fusion | flops 3326202880 | bytes 12130304 | tf_op jit(solution)/shard_map/dot_general | solution.py:64
  496.1 28.4 %pmax.7 = bf16[704,16]{0,1:T(8,128)(2,1)S(1)} all-reduce(bf16[704,16]{0,1:T(8,128)(2,1)S(1)} %get-tuple-element.11), channel_id=1, replica_groups=mesh['expert'=64,'replica'=8] {'replica'}, use_global_device_ids=true, to_apply=%region_6.7 | all-reduce | flops 11264 | bytes 45056 | tf_op jit(solution)/shard_map/pmax | solution.py:69
  524.5 4.3 divide_convert_fusion
  532.2 5.5 convert_element_type.82
  541.6 6.8 %fusion.4 = f32[1152]{0:T(1024)S(1)} fusion(bf16[1152,704]{0,1:T(8,128)(2,1)} %copy.27, bf16[1152,2048]{1,0:T(8,128)(2,1)} %reshape.120, bf16[1,704,2048]{2,1,0:T(8,128)(2,1)S(1)} %copy-done), kind=kOutput, calls=%fused_computation.13 | convolution fusion | flops 3324320768 | bytes 9228800 | tf_op jit(solution)/shard_map/dot_general | solution.py:52
  549.1 6.9 %all-to-all-start.2 = ((f32[64,1,18]{2,1,0:T(1,128)}), f32[64,1,18]{2,1,0:T(1,128)S(1)}, u32[]{:S(2)}, u32[]{:S(2)}) async-start(f32[64,1,18]{2,1,0:T(1,128)} %bitcast.2), calls=%async_computation.2 | async-start | bytes 65536 | tf_op jit(solution)/shard_map/all_to_all | solution.py:57
  556.7 12.7 %all-to-all-done.2 = f32[64,1,18]{2,1,0:T(1,128)S(1)} async-done(((f32[64,1,18]{2,1,0:T(1,128)}), f32[64,1,18]{2,1,0:T(1,128)S(1)}, u32[]{:S(2)}, u32[]{:S(2)}) %all-to-all-start.2) | async-done | bytes 4640 | tf_op jit(solution)/shard_map/all_to_all | solution.py:57
  570.8 4.5 gather_fusion.2
  576.0 74.6 %all-gather.2.cloned.1.call-done = bf16[8,704,2048]{2,1,0:T(8,128)(2,1)} async-done(((bf16[1,704,2048]{2,1,0:T(8,128)(2,1)}), bf16[8,704,2048]{2,1,0:T(8,128)(2,1)}) %all-gather.2.cloned.1.call-update) | async-done | bytes 23068688 | tf_op jit(solution)/shard_map/all_gather | solution.py:76
  650.7 14.6 %reduce_sum.35 = bf16[704,2048]{1,0:T(8,128)(2,1)} reduce(bf16[8,704,2048]{2,1,0:T(8,128)(2,1)} %all-gather.2.cloned.1.call-done, bf16[]{:T(256)} %constant.19.clone.1), dimensions={0}, to_apply=%region_7.8 | reduce | flops 10092544 | bytes 25952258 | tf_op jit(solution)/shard_map/reduce_sum | solution.py:76
  (44 shorter events, 32.7 us)
Async XLA Ops:
  7.2 534.4 %copy-start = (bf16[1,704,2048]{2,1,0:T(8,128)(2,1)S(1)}, bf16[1,704,2048]{2,1,0:T(8,128)(2,1)}, u32[]{:S(2)}) copy-start(bf16[1,704,2048]{2,1,0:T(8,128)(2,1)} %param.9) | copy-start | bytes 8650756
  24.2 39.2 %all-to-all-start.3 = ((bf16[64,1,18]{2,1,0:T(2,128)(2,1)}), bf16[64,1,18]{2,1,0:T(2,128)(2,1)S(1)}, u32[]{:S(2)}, u32[]{:S(2)}) async-start(bf16[64,1,18]{2,1,0:T(2,128)(2,1)} %convert_element_type.85), calls=%async_computation.3 | async-start | bytes 65536 | tf_op jit(solution)/shard_map/all_to_all | solution.py:46
  63.4 120.1 %all-to-all-start.1 = ((bf16[64,18,704]{2,1,0:T(8,128)(2,1)}), bf16[64,18,704]{2,1,0:T(8,128)(2,1)}, u32[]{:S(2)}, u32[]{:S(2)}) async-start(bf16[64,18,704]{2,1,0:T(8,128)(2,1)} %reshape.122), calls=%async_computation.1 | async-start | bytes 4718592 | tf_op jit(solution)/shard_map/all_to_all | solution.py:49
  183.5 283.7 %all-to-all-start = ((bf16[64,18,2048]{2,1,0:T(8,128)(2,1)}), bf16[64,18,2048]{2,1,0:T(8,128)(2,1)}, u32[]{:S(2)}, u32[]{:S(2)}) async-start(bf16[64,18,2048]{2,1,0:T(8,128)(2,1)} %reshape.119), calls=%async_computation | async-start | bytes 12582912 | tf_op jit(solution)/shard_map/all_to_all | solution.py:45
  194.6 456.0 %all-gather.2.cloned.1.call-start = ((), (), s32[]{:S(2)}) async-start(), calls=%async_computation.4 | async-start | bytes 25952256 | tf_op jit(solution)/shard_map/all_gather | solution.py:76
  549.1 20.3 %all-to-all-start.2 = ((f32[64,1,18]{2,1,0:T(1,128)}), f32[64,1,18]{2,1,0:T(1,128)S(1)}, u32[]{:S(2)}, u32[]{:S(2)}) async-start(f32[64,1,18]{2,1,0:T(1,128)} %bitcast.2), calls=%async_computation.2 | async-start | bytes 65536 | tf_op jit(solution)/shard_map/all_to_all | solution.py:57
Sparse Core Ops, SparseCore 0:
  537.8 112.7 all-gather.1
